TPU v7x, 32 devices: a whole 2x2x4 slice. The times are simulated.
32 devices in a mesh: section: 4 (over y, x), tp: 8 (over z, core).
Axes of the slice: x: 2, y: 2, z: 4, core: 2. Of those that a mesh axis runs over, the one named last changes fastest.
Arguments:
- entering: bfloat16 [2, 3, 32, 4096], P(None, None, None, 'tp'), may hold values from -6 to 6
- output_grad: bfloat16 [2, 3, 32, 4096], P(None, None, None, 'tp'), may hold values from -6 to 6
- live_counts: int32 [2, 3], replicated, may hold values from 1 to 32, as said below
- segment_ids: int32 [2, 3, 32], replicated, may hold values from 0 to 3, never falling along the last dimension, each value on 1 to 16 neighbouring positions
- weight_in: bfloat16 [4, 4096, 11008], P('section', None, 'tp'), may hold values from -0.125 to 0.125
- weight_out: bfloat16 [4, 11008, 4096], P('section', 'tp'), may hold values from -0.078125 to 0.078125
- norm_gain: bfloat16 [4, 4096], P('section'), may hold values from 0.25 to 1.75
- shift_mix: bfloat16 [4, 4096], P('section'), may hold values from 0.099609375 to 0.8984375
Outputs:
- grad_in: bfloat16 [4, 4096, 11008], P('section', None, 'tp')
- grad_out: bfloat16 [4, 11008, 4096], P('section', 'tp')
- grad_gain: float32 [4, 4096], P('section', 'tp')
- grad_mix: float32 [4, 4096], P('section', 'tp')
Inputs may be any that keep to these rules, and one draw needn't show every extreme that they name: `live_counts`: in each relay at least one micro-batch has all 32 rows live. `segment_ids`: never falls along the rows of a micro-batch.
All inputs are finite; a program needn't handle non-finite values.
Results may differ from a plain program's by a relative error of at most 0.03.
Values may be sent and summed in bfloat16 or wider, within the bound.
A program may use at most 256 MiB of HBM per device.

v0:
```python
import jax
import jax.numpy as jnp
from jax import lax
from jax.sharding import PartitionSpec as P

epsilon = 1e-05


def shortened(value):
    return jax.tree.map(lambda a: a.astype(jnp.bfloat16) if a.dtype == jnp.float32 else a, value)


def passed_along(value, axis, steps):
    count = lax.axis_size(axis)
    leading, last = (max(0, -steps), min(count, count - steps))
    return lax.ppermute(value, axis, [(source, source + steps) for source in range(leading, last)])


def row_linkage(segment_ids):
    joined = segment_ids[..., 1:] == segment_ids[..., :-1]
    leading = jnp.zeros(segment_ids.shape[:-1] + (1,), jnp.float32)
    return jnp.concatenate([leading, joined.astype(jnp.float32)], axis=-1)


def earlier_rows(values, linkage):
    shifted = jnp.concatenate([jnp.zeros_like(values[..., :1, :]), values[..., :-1, :]], axis=-2)
    return shifted * linkage[..., None]


def later_rows(values, linkage):
    shifted = values[..., 1:, :] * linkage[..., 1:, None]
    return jnp.concatenate([shifted, jnp.zeros_like(values[..., :1, :])], axis=-2)


def silu_slope(pre_act):
    sigmoid = jax.nn.sigmoid(pre_act)
    return sigmoid * (1.0 + pre_act * (1.0 - sigmoid))


def rounded(values):
    return lax.optimization_barrier(values.astype(jnp.bfloat16)).astype(jnp.float32)


def mixed_rows(inputs, linkage, mix_values):
    floats = inputs.astype(jnp.float32)
    earlier = earlier_rows(floats, linkage)
    return (floats, earlier, floats + mix_values * (earlier - floats))


def write_slot(buffer, relay, slot_index, active_now, values):
    current = buffer[relay, slot_index]
    return buffer.at[relay, slot_index].set(jnp.where(active_now, values, current))


def local(
    entering, output_grad, live_counts, segment_ids, weight_in, weight_out, norm_gain, shift_mix
):
    phases = lax.axis_size("section")
    position = lax.axis_index("section")
    tp_index = lax.axis_index("tp")
    micro_count = entering.shape[1]
    tok_rows = entering.shape[2]
    width_local = entering.shape[3]
    width_all = weight_in.shape[1]
    hidden_local = weight_in.shape[2]
    start_local = tp_index * width_local
    linkage = row_linkage(segment_ids)
    row_index = jnp.arange(tok_rows)
    live_rows = (row_index[None, None, :] < live_counts[..., None]).astype(jnp.float32)
    upstream_all = (output_grad.astype(jnp.float32) * live_rows[..., None]).astype(jnp.bfloat16)
    own_first = weight_in[0]
    own_second = weight_out[0]
    own_gain = norm_gain[0]
    own_mix = shift_mix[0]
    firsts = [own_first, own_first]
    seconds = [own_second, own_second]
    gain_full = [own_gain.astype(jnp.float32), own_gain.astype(jnp.float32)]
    mix_full = [own_mix.astype(jnp.float32), own_mix.astype(jnp.float32)]
    positions = [position, position]
    gain_part = [lax.dynamic_slice_in_dim(values, start_local, width_local) for values in gain_full]
    mix_part = [lax.dynamic_slice_in_dim(values, start_local, width_local) for values in mix_full]
    tick_count = micro_count + phases - 1

    def forward_tick(tick_index, loop_state):
        received, input_buffer, normed_buffer, summed_buffer, scale_buffer, hidden_buffer = (
            loop_state
        )
        shards, active_list, slot_list = ([], [], [])
        for relay in range(2):
            slot_index = tick_index - positions[relay]
            active_now = (slot_index >= 0) & (slot_index < micro_count)
            slot_index = jnp.clip(slot_index, 0, micro_count - 1)
            entering_rows = entering[relay, slot_index]
            shards.append(jnp.where(positions[relay] == 0, entering_rows, received[relay]))
            active_list.append(active_now)
            slot_list.append(slot_index)
        whole = lax.all_gather(shortened(jnp.stack(shards)), "tp", axis=2, tiled=True)
        partial_list = []
        for relay in range(2):
            active_now = active_list[relay]
            slot_index = slot_list[relay]
            row_link = linkage[relay, slot_index]
            floats, earlier, united = mixed_rows(whole[relay], row_link, mix_full[relay])
            row_scale = lax.rsqrt(jnp.sum(united * united, axis=-1) / width_all + epsilon)
            normed = (united * gain_full[relay]).astype(jnp.bfloat16)
            first_weights = firsts[relay]
            second_weights = seconds[relay]
            summed = lax.cond(
                active_now,
                lambda: jnp.dot(normed, first_weights, preferred_element_type=jnp.float32),
                lambda: jnp.zeros((tok_rows, hidden_local), jnp.float32),
            )
            hidden = jax.nn.silu(row_scale[:, None] * summed).astype(jnp.bfloat16)
            partial_value = lax.cond(
                active_now,
                lambda: jnp.dot(hidden, second_weights, preferred_element_type=jnp.float32),
                lambda: jnp.zeros((tok_rows, width_all), jnp.float32),
            )
            partial_list.append(partial_value)
            input_buffer = write_slot(input_buffer, relay, slot_index, active_now, shards[relay])
            normed_buffer = write_slot(normed_buffer, relay, slot_index, active_now, normed)
            summed_buffer = write_slot(summed_buffer, relay, slot_index, active_now, summed)
            scale_buffer = write_slot(scale_buffer, relay, slot_index, active_now, row_scale)
            hidden_buffer = write_slot(hidden_buffer, relay, slot_index, active_now, hidden)
        sums = lax.psum_scatter(
            jnp.stack(partial_list).astype(jnp.bfloat16), "tp", scatter_dimension=2, tiled=True
        ).astype(jnp.float32)
        outputs = [
            (shards[relay].astype(jnp.float32) + sums[relay]).astype(jnp.bfloat16)
            for relay in range(2)
        ]
        received = passed_along(jnp.stack(outputs), "section", 1)
        return (received, input_buffer, normed_buffer, summed_buffer, scale_buffer, hidden_buffer)

    forward_start = (
        jnp.zeros((2, tok_rows, width_local), jnp.bfloat16),
        jnp.zeros((2, micro_count, tok_rows, width_local), jnp.bfloat16),
        jnp.zeros((2, micro_count, tok_rows, width_all), jnp.bfloat16),
        jnp.zeros((2, micro_count, tok_rows, hidden_local), jnp.float32),
        jnp.zeros((2, micro_count, tok_rows), jnp.float32),
        jnp.zeros((2, micro_count, tok_rows, hidden_local), jnp.bfloat16),
    )
    forward_state = lax.fori_loop(0, tick_count, forward_tick, forward_start)
    input_buffer, normed_buffer, summed_buffer, scale_buffer, hidden_buffer = forward_state[1:]

    def backward_tick(tick_index, loop_state):
        received, upstream_buffer, gate_buffer, gain_sums, mix_sums = loop_state
        shards, active_list, slot_list = ([], [], [])
        for relay in range(2):
            slot_index = tick_index - (phases - 1 - positions[relay])
            active_now = (slot_index >= 0) & (slot_index < micro_count)
            slot_index = jnp.clip(slot_index, 0, micro_count - 1)
            entering_rows = upstream_all[relay, slot_index]
            shards.append(jnp.where(positions[relay] == phases - 1, entering_rows, received[relay]))
            active_list.append(active_now)
            slot_list.append(slot_index)
        whole_up = lax.all_gather(shortened(jnp.stack(shards)), "tp", axis=2, tiled=True)
        rate_list, summed_grads, scale_list = ([], [], [])
        for relay in range(2):
            active_now = active_list[relay]
            slot_index = slot_list[relay]
            second_weights = seconds[relay]
            upstream_rows = whole_up[relay]
            grad_hidden = lax.cond(
                active_now,
                lambda: lax.dot_general(
                    upstream_rows,
                    second_weights,
                    (((1,), (1,)), ((), ())),
                    preferred_element_type=jnp.float32,
                ),
                lambda: jnp.zeros((tok_rows, hidden_local), jnp.float32),
            )
            summed = summed_buffer[relay, slot_index]
            row_scale = scale_buffer[relay, slot_index]
            gate_grad = grad_hidden * silu_slope(row_scale[:, None] * summed)
            grad_summed = (gate_grad * row_scale[:, None]).astype(jnp.bfloat16)
            rate_list.append(jnp.sum(gate_grad * summed, axis=-1))
            summed_grads.append(grad_summed)
            scale_list.append(row_scale)
            upstream_buffer = write_slot(
                upstream_buffer, relay, slot_index, active_now, upstream_rows
            )
            gate_buffer = write_slot(gate_buffer, relay, slot_index, active_now, grad_summed)
        grad_rate = lax.psum(jnp.stack(rate_list), "tp")
        partial_list = []
        for relay in range(2):
            first_weights = firsts[relay]
            gate_rows = summed_grads[relay]
            partial_value = lax.cond(
                active_list[relay],
                lambda: lax.dot_general(
                    gate_rows,
                    first_weights,
                    (((1,), (1,)), ((), ())),
                    preferred_element_type=jnp.float32,
                ),
                lambda: jnp.zeros((tok_rows, width_all), jnp.float32),
            )
            partial_list.append(partial_value)
        grad_normed_all = lax.psum_scatter(
            jnp.stack(partial_list).astype(jnp.bfloat16), "tp", scatter_dimension=2, tiled=True
        ).astype(jnp.float32)
        outputs = []
        for relay in range(2):
            slot_index = slot_list[relay]
            row_link = linkage[relay, slot_index]
            floats, earlier, united = mixed_rows(
                input_buffer[relay, slot_index], row_link, mix_part[relay]
            )
            grad_normed = grad_normed_all[relay]
            factor = grad_rate[relay] * scale_list[relay] ** 3 / width_all
            grad_united = grad_normed * gain_part[relay] - factor[:, None] * united
            weight_live = active_list[relay].astype(jnp.float32)
            gain_sums = gain_sums.at[relay].add(weight_live * jnp.sum(grad_normed * united, axis=0))
            mix_sums = mix_sums.at[relay].add(
                weight_live * jnp.sum(grad_united * (earlier - floats), axis=0)
            )
            below = (
                shards[relay].astype(jnp.float32)
                + grad_united * (1.0 - mix_part[relay])
                + later_rows(grad_united * mix_part[relay], row_link)
            )
            outputs.append(below.astype(jnp.bfloat16))
        received = passed_along(shortened(jnp.stack(outputs)), "section", -1)
        return (received, upstream_buffer, gate_buffer, gain_sums, mix_sums)

    backward_start = (
        jnp.zeros((2, tok_rows, width_local), jnp.bfloat16),
        jnp.zeros((2, micro_count, tok_rows, width_all), jnp.bfloat16),
        jnp.zeros((2, micro_count, tok_rows, hidden_local), jnp.bfloat16),
        jnp.zeros((2, width_local), jnp.float32),
        jnp.zeros((2, width_local), jnp.float32),
    )
    backward_state = lax.fori_loop(0, tick_count, backward_tick, backward_start)
    upstream_buffer, gate_buffer, gain_sums, mix_sums = backward_state[1:]
    first_grads, second_grads = ([], [])
    for relay in range(2):
        normed_rows = normed_buffer[relay].reshape(-1, width_all)
        gate_rows = gate_buffer[relay].reshape(-1, hidden_local)
        first_grads.append(
            lax.dot_general(
                normed_rows, gate_rows, (((0,), (0,)), ((), ())), preferred_element_type=jnp.float32
            )
        )
        hidden_rows = hidden_buffer[relay].reshape(-1, hidden_local)
        upstream_rows = upstream_buffer[relay].reshape(-1, width_all)
        second_grads.append(
            lax.dot_general(
                hidden_rows,
                upstream_rows,
                (((0,), (0,)), ((), ())),
                preferred_element_type=jnp.float32,
            )
        )
    other_first = rounded(first_grads[1])
    other_second = rounded(second_grads[1])
    other_gain = rounded(gain_sums[1])
    other_mix = rounded(mix_sums[1])
    grad_in = (rounded(first_grads[0]) + other_first).astype(jnp.bfloat16)[None]
    grad_out = (rounded(second_grads[0]) + other_second).astype(jnp.bfloat16)[None]
    grad_gain = (rounded(gain_sums[0]) + other_gain)[None]
    grad_mix = (rounded(mix_sums[0]) + other_mix)[None]
    return (grad_in, grad_out, grad_gain, grad_mix)


def solution(mesh):
    in_specs = (
        P(None, None, None, "tp"),
        P(None, None, None, "tp"),
        P(),
        P(),
        P("section", None, "tp"),
        P("section", "tp", None),
        P("section", None),
        P("section", None),
    )
    out_specs = (
        P("section", None, "tp"),
        P("section", "tp", None),
        P("section", "tp"),
        P("section", "tp"),
    )
    return jax.shard_map(local, mesh=mesh, in_specs=in_specs, out_specs=out_specs, check_vma=False)
```

profile of v0, /device:TPU:0, one launch (start us, length us, event | category | flops | bytes accessed | tf_op | source)
XLA Modules:
  0.0 1122.2 jit_solution(11325779443382251624)
XLA Ops:
  12.0 15.3 %copy.14 = bf16[1,4096,1376]{2,1,0:T(8,128)(2,1)} copy(bf16[1,4096,1376]{1,2,0:T(8,128)(2,1)} %param.68) | data formatting | bytes 22544384 | tf_op args[4]
  28.9 515.0 %while.68 = (s32[]{:T(128)}, bf16[2,32,512]{2,1,0:T(8,128)(2,1)S(1)}, bf16[2,3,32,512]{3,2,1,0:T(8,128)(2,1)S(1)}, bf16[2,3,32,4096]{3,2,1,0:T(8,128)(2,1)}, f32...) while((s32[]{:T(128)}, ...), condition=%wide.region_16.17_spmd, body=%wide.region_0.16_spmd.sunk | while | flops 1448767872 | bytes 63949388 | solution.py:143
  30.0 16.6 %all_gather.22 = bf16[2,32,4096]{2,1,0:T(8,128)(2,1)S(1)} all-gather(bf16[2,32,512]{2,1,0:T(8,128)(2,1)S(1)} %pad_maximum_fusion.14), channel_id=1, replica_groups=mesh['section'=4,'tp'=8] {'tp'}, dimensions={2}, use_global_device_ids=true | all-gather | bytes 589824 | tf_op jit(solution)/shard_map/while/body/eval_jaxpr/all_gather | solution.py:97
  84.0 26.0 %reduce-scatter.3.cloned.1.call-done = bf16[2,32,512]{2,1,0:T(8,128)(2,1)} async-done(((bf16[2,32,4096]{2,1,0:T(8,128)(2,1)}), bf16[2,32,512]{2,1,0:T(8,128)(2,1)}) %reduce-scatter.3.cloned.1.call-update) | async-done | bytes 65552 | tf_op jit(solution)/shard_map/while/body/eval_jaxpr/reduce_scatter | solution.py:125
  117.3 14.8 %all_gather.22 = bf16[2,32,4096]{2,1,0:T(8,128)(2,1)S(1)} all-gather(bf16[2,32,512]{2,1,0:T(8,128)(2,1)S(1)} %pad_maximum_fusion.14), channel_id=1, replica_groups=mesh['section'=4,'tp'=8] {'tp'}, dimensions={2}, use_global_device_ids=true | all-gather | bytes 589824 | tf_op jit(solution)/shard_map/while/body/eval_jaxpr/all_gather | solution.py:97
  169.6 25.3 %reduce-scatter.3.cloned.1.call-done = bf16[2,32,512]{2,1,0:T(8,128)(2,1)} async-done(((bf16[2,32,4096]{2,1,0:T(8,128)(2,1)}), bf16[2,32,512]{2,1,0:T(8,128)(2,1)}) %reduce-scatter.3.cloned.1.call-update) | async-done | bytes 65552 | tf_op jit(solution)/shard_map/while/body/eval_jaxpr/reduce_scatter | solution.py:125
  202.1 14.9 %all_gather.22 = bf16[2,32,4096]{2,1,0:T(8,128)(2,1)S(1)} all-gather(bf16[2,32,512]{2,1,0:T(8,128)(2,1)S(1)} %pad_maximum_fusion.14), channel_id=1, replica_groups=mesh['section'=4,'tp'=8] {'tp'}, dimensions={2}, use_global_device_ids=true | all-gather | bytes 589824 | tf_op jit(solution)/shard_map/while/body/eval_jaxpr/all_gather | solution.py:97
  254.4 26.2 %reduce-scatter.3.cloned.1.call-done = bf16[2,32,512]{2,1,0:T(8,128)(2,1)} async-done(((bf16[2,32,4096]{2,1,0:T(8,128)(2,1)}), bf16[2,32,512]{2,1,0:T(8,128)(2,1)}) %reduce-scatter.3.cloned.1.call-update) | async-done | bytes 65552 | tf_op jit(solution)/shard_map/while/body/eval_jaxpr/reduce_scatter | solution.py:125
  287.7 14.9 %all_gather.22 = bf16[2,32,4096]{2,1,0:T(8,128)(2,1)S(1)} all-gather(bf16[2,32,512]{2,1,0:T(8,128)(2,1)S(1)} %pad_maximum_fusion.14), channel_id=1, replica_groups=mesh['section'=4,'tp'=8] {'tp'}, dimensions={2}, use_global_device_ids=true | all-gather | bytes 589824 | tf_op jit(solution)/shard_map/while/body/eval_jaxpr/all_gather | solution.py:97
  315.2 51.1 %reduce-scatter.3.cloned.1.call-done = bf16[2,32,512]{2,1,0:T(8,128)(2,1)} async-done(((bf16[2,32,4096]{2,1,0:T(8,128)(2,1)}), bf16[2,32,512]{2,1,0:T(8,128)(2,1)}) %reduce-scatter.3.cloned.1.call-update) | async-done | bytes 65552 | tf_op jit(solution)/shard_map/while/body/eval_jaxpr/reduce_scatter | solution.py:125
  373.4 14.9 %all_gather.22 = bf16[2,32,4096]{2,1,0:T(8,128)(2,1)S(1)} all-gather(bf16[2,32,512]{2,1,0:T(8,128)(2,1)S(1)} %pad_maximum_fusion.14), channel_id=1, replica_groups=mesh['section'=4,'tp'=8] {'tp'}, dimensions={2}, use_global_device_ids=true | all-gather | bytes 589824 | tf_op jit(solution)/shard_map/while/body/eval_jaxpr/all_gather | solution.py:97
  401.0 51.0 %reduce-scatter.3.cloned.1.call-done = bf16[2,32,512]{2,1,0:T(8,128)(2,1)} async-done(((bf16[2,32,4096]{2,1,0:T(8,128)(2,1)}), bf16[2,32,512]{2,1,0:T(8,128)(2,1)}) %reduce-scatter.3.cloned.1.call-update) | async-done | bytes 65552 | tf_op jit(solution)/shard_map/while/body/eval_jaxpr/reduce_scatter | solution.py:125
  459.2 14.9 %all_gather.22 = bf16[2,32,4096]{2,1,0:T(8,128)(2,1)S(1)} all-gather(bf16[2,32,512]{2,1,0:T(8,128)(2,1)S(1)} %pad_maximum_fusion.14), channel_id=1, replica_groups=mesh['section'=4,'tp'=8] {'tp'}, dimensions={2}, use_global_device_ids=true | all-gather | bytes 589824 | tf_op jit(solution)/shard_map/while/body/eval_jaxpr/all_gather | solution.py:97
  486.7 51.0 %reduce-scatter.3.cloned.1.call-done = bf16[2,32,512]{2,1,0:T(8,128)(2,1)} async-done(((bf16[2,32,4096]{2,1,0:T(8,128)(2,1)}), bf16[2,32,512]{2,1,0:T(8,128)(2,1)}) %reduce-scatter.3.cloned.1.call-update) | async-done | bytes 65552 | tf_op jit(solution)/shard_map/while/body/eval_jaxpr/reduce_scatter | solution.py:125
  546.1 521.7 %while.69 = (s32[]{:T(128)}, bf16[2,32,512]{2,1,0:T(8,128)(2,1)S(1)}, bf16[2,3,32,4096]{3,2,1,0:T(8,128)(2,1)}, bf16[2,3,32,1376]{3,2,1,0:T(8,128)(2,1)S(1)}, f3...) while((s32[]{:T(128)}, ...), condition=%wide.region_36.37_spmd, body=%wide.region_17.36_spmd.sunk | while | flops 1445767936 | bytes 57990940 | solution.py:235
  546.9 15.0 %all_gather.23 = bf16[2,32,4096]{2,1,0:T(8,128)(2,1)S(1)} all-gather(bf16[2,32,512]{2,1,0:T(8,128)(2,1)S(1)} %pad_maximum_fusion.17), channel_id=1, replica_groups=mesh['section'=4,'tp'=8] {'tp'}, dimensions={2}, use_global_device_ids=true | all-gather | bytes 589824 | tf_op jit(solution)/shard_map/while/body/eval_jaxpr/all_gather | solution.py:157
  584.5 41.6 %reduce-scatter.5.cloned.1.call-done = bf16[2,32,512]{2,1,0:T(8,128)(2,1)} async-done(((bf16[2,32,4096]{2,1,0:T(8,128)(2,1)}), bf16[2,32,512]{2,1,0:T(8,128)(2,1)}) %reduce-scatter.5.cloned.1.call-update) | async-done | bytes 65552 | tf_op jit(solution)/shard_map/while/body/eval_jaxpr/reduce_scatter | solution.py:201
  635.1 14.9 %all_gather.23 = bf16[2,32,4096]{2,1,0:T(8,128)(2,1)S(1)} all-gather(bf16[2,32,512]{2,1,0:T(8,128)(2,1)S(1)} %pad_maximum_fusion.17), channel_id=1, replica_groups=mesh['section'=4,'tp'=8] {'tp'}, dimensions={2}, use_global_device_ids=true | all-gather | bytes 589824 | tf_op jit(solution)/shard_map/while/body/eval_jaxpr/all_gather | solution.py:157
  672.8 39.6 %reduce-scatter.5.cloned.1.call-done = bf16[2,32,512]{2,1,0:T(8,128)(2,1)} async-done(((bf16[2,32,4096]{2,1,0:T(8,128)(2,1)}), bf16[2,32,512]{2,1,0:T(8,128)(2,1)}) %reduce-scatter.5.cloned.1.call-update) | async-done | bytes 65552 | tf_op jit(solution)/shard_map/while/body/eval_jaxpr/reduce_scatter | solution.py:201
  721.5 14.8 %all_gather.23 = bf16[2,32,4096]{2,1,0:T(8,128)(2,1)S(1)} all-gather(bf16[2,32,512]{2,1,0:T(8,128)(2,1)S(1)} %pad_maximum_fusion.17), channel_id=1, replica_groups=mesh['section'=4,'tp'=8] {'tp'}, dimensions={2}, use_global_device_ids=true | all-gather | bytes 589824 | tf_op jit(solution)/shard_map/while/body/eval_jaxpr/all_gather | solution.py:157
  759.1 40.5 %reduce-scatter.5.cloned.1.call-done = bf16[2,32,512]{2,1,0:T(8,128)(2,1)} async-done(((bf16[2,32,4096]{2,1,0:T(8,128)(2,1)}), bf16[2,32,512]{2,1,0:T(8,128)(2,1)}) %reduce-scatter.5.cloned.1.call-update) | async-done | bytes 65552 | tf_op jit(solution)/shard_map/while/body/eval_jaxpr/reduce_scatter | solution.py:201
  808.7 14.9 %all_gather.23 = bf16[2,32,4096]{2,1,0:T(8,128)(2,1)S(1)} all-gather(bf16[2,32,512]{2,1,0:T(8,128)(2,1)S(1)} %pad_maximum_fusion.17), channel_id=1, replica_groups=mesh['section'=4,'tp'=8] {'tp'}, dimensions={2}, use_global_device_ids=true | all-gather | bytes 589824 | tf_op jit(solution)/shard_map/while/body/eval_jaxpr/all_gather | solution.py:157
  896.0 14.9 %all_gather.23 = bf16[2,32,4096]{2,1,0:T(8,128)(2,1)S(1)} all-gather(bf16[2,32,512]{2,1,0:T(8,128)(2,1)S(1)} %pad_maximum_fusion.17), channel_id=1, replica_groups=mesh['section'=4,'tp'=8] {'tp'}, dimensions={2}, use_global_device_ids=true | all-gather | bytes 589824 | tf_op jit(solution)/shard_map/while/body/eval_jaxpr/all_gather | solution.py:157
  983.3 14.9 %all_gather.23 = bf16[2,32,4096]{2,1,0:T(8,128)(2,1)S(1)} all-gather(bf16[2,32,512]{2,1,0:T(8,128)(2,1)S(1)} %pad_maximum_fusion.17), channel_id=1, replica_groups=mesh['section'=4,'tp'=8] {'tp'}, dimensions={2}, use_global_device_ids=true | all-gather | bytes 589824 | tf_op jit(solution)/shard_map/while/body/eval_jaxpr/all_gather | solution.py:157
  (604 shorter events, 724.2 us)
Async XLA Ops:
  28.9 81.1 %reduce-scatter.3.cloned.1.call-start = ((), (), s32[]{:S(2)}) async-start(), calls=%async_computation.2 | async-start | bytes 589824 | tf_op jit(solution)/shard_map/while/body/eval_jaxpr/reduce_scatter | solution.py:125
  110.9 5.3 collective-permute-start
  116.2 78.6 %reduce-scatter.3.cloned.1.call-start = ((), (), s32[]{:S(2)}) async-start(), calls=%async_computation.2 | async-start | bytes 589824 | tf_op jit(solution)/shard_map/while/body/eval_jaxpr/reduce_scatter | solution.py:125
  195.7 5.3 collective-permute-start
  201.0 79.5 %reduce-scatter.3.cloned.1.call-start = ((), (), s32[]{:S(2)}) async-start(), calls=%async_computation.2 | async-start | bytes 589824 | tf_op jit(solution)/shard_map/while/body/eval_jaxpr/reduce_scatter | solution.py:125
  281.5 5.2 collective-permute-start
  286.7 79.6 %reduce-scatter.3.cloned.1.call-start = ((), (), s32[]{:S(2)}) async-start(), calls=%async_computation.2 | async-start | bytes 589824 | tf_op jit(solution)/shard_map/while/body/eval_jaxpr/reduce_scatter | solution.py:125
  367.2 5.2 collective-permute-start
  372.4 79.6 %reduce-scatter.3.cloned.1.call-start = ((), (), s32[]{:S(2)}) async-start(), calls=%async_computation.2 | async-start | bytes 589824 | tf_op jit(solution)/shard_map/while/body/eval_jaxpr/reduce_scatter | solution.py:125
  452.8 5.3 collective-permute-start
  458.2 79.5 %reduce-scatter.3.cloned.1.call-start = ((), (), s32[]{:S(2)}) async-start(), calls=%async_computation.2 | async-start | bytes 589824 | tf_op jit(solution)/shard_map/while/body/eval_jaxpr/reduce_scatter | solution.py:125
  538.6 5.3 collective-permute-start
  546.1 80.0 %reduce-scatter.5.cloned.1.call-start = ((), (), s32[]{:S(2)}) async-start(), calls=%async_computation.3 | async-start | bytes 589824 | tf_op jit(solution)/shard_map/while/body/eval_jaxpr/reduce_scatter | solution.py:201
  628.1 6.2 collective-permute-start.1
  634.2 78.1 %reduce-scatter.5.cloned.1.call-start = ((), (), s32[]{:S(2)}) async-start(), calls=%async_computation.3 | async-start | bytes 589824 | tf_op jit(solution)/shard_map/while/body/eval_jaxpr/reduce_scatter | solution.py:201
  714.5 6.2 collective-permute-start.1
  720.6 79.0 %reduce-scatter.5.cloned.1.call-start = ((), (), s32[]{:S(2)}) async-start(), calls=%async_computation.3 | async-start | bytes 589824 | tf_op jit(solution)/shard_map/while/body/eval_jaxpr/reduce_scatter | solution.py:201
  801.7 6.2 collective-permute-start.1
  807.9 79.0 %reduce-scatter.5.cloned.1.call-start = ((), (), s32[]{:S(2)}) async-start(), calls=%async_computation.3 | async-start | bytes 589824 | tf_op jit(solution)/shard_map/while/body/eval_jaxpr/reduce_scatter | solution.py:201
  889.0 6.2 collective-permute-start.1
  895.1 79.1 %reduce-scatter.5.cloned.1.call-start = ((), (), s32[]{:S(2)}) async-start(), calls=%async_computation.3 | async-start | bytes 589824 | tf_op jit(solution)/shard_map/while/body/eval_jaxpr/reduce_scatter | solution.py:201
  976.3 6.2 collective-permute-start.1
  982.4 77.1 %reduce-scatter.5.cloned.1.call-start = ((), (), s32[]{:S(2)}) async-start(), calls=%async_computation.3 | async-start | bytes 589824 | tf_op jit(solution)/shard_map/while/body/eval_jaxpr/reduce_scatter | solution.py:201
  1061.6 6.2 collective-permute-start.1
  (6 other events, 60.3 us)
Sparse Core Ops, SparseCore 0:
  79.9 30.0 reduce-scatter.2
  165.5 29.3 reduce-scatter.2
  250.3 30.2 reduce-scatter.2
  311.1 55.1 reduce-scatter.2
  396.9 55.0 reduce-scatter.2
  482.6 55.0 reduce-scatter.2
  565.5 60.4 reduce-scatter.4
  653.5 58.7 reduce-scatter.4
  739.9 59.6 reduce-scatter.4
  857.5 29.3 reduce-scatter.4
  944.9 29.3 reduce-scatter.4
  1032.1 27.4 reduce-scatter.4
where the time goes:
time: 1130 us; the launch traced here: 1120 us
  waiting for transfers between devices  417 us (37%)
  blocking collectives  266 us (24%)
  matrix products  189 us (17%)
  other arithmetic  169 us (15%)
  local copies, waits for them, and re-layouts  35.2 us (3%)
  starting transfers between devices  28.1 us (2%)
  between operations  14.1 us (1%)
    reduce_scatter x6, waiting for transfers between devices, forward_tick(): lax.psum_scatter(jnp.stack(partial_list).astype(jnp.bfloat16), 'tp', scat...  231 us
    reduce_scatter x6, waiting for transfers between devices, backward_tick(): lax.psum_scatter(jnp.stack(partial_list).astype(jnp.bfloat16), 'tp', scat...  150 us
    all_gather x6, blocking collectives, forward_tick(): lax.all_gather(shortened(jnp.stack(shards)), 'tp', axis=2, tiled=True)  90.9 us
    all_gather x6, blocking collectives, backward_tick(): lax.all_gather(shortened(jnp.stack(shards)), 'tp', axis=2, tiled=True)  89.3 us
    psum x6, blocking collectives, backward_tick(): grad_rate = lax.psum(jnp.stack(rate_list), 'tp')  85.8 us
    scatter x72, other arithmetic, write_slot(): buffer.at[relay, slot_index].set(jnp.where(active_now, values, current))  83 us
    dot_general x6, matrix products, backward_tick(): lax.dot_general(gate_rows, first_weights, (((1,), (1,)), ((), ())), prefe...  46.1 us
    dot_general x6, matrix products, backward_tick(): lax.dot_general(upstream_rows, second_weights, (((1,), (1,)), ((), ())),...  45.2 us
  transfers between devices with their start and end apart: 24, of which 24 were waited for; matrix products, arithmetic and copies ran while one was open for 5% of the time, Pallas kernels for 0%

commit v1 on v0

v1 whole, which is shorter than its diff:
```python
import functools

import jax
import jax.numpy as jnp
from jax import lax
from jax.experimental import pallas as pl
from jax.experimental.pallas import tpu as pltpu
from jax.sharding import PartitionSpec as P

epsilon = 1e-05
MESH = pl.DeviceIdType.MESH
NT = (((1,), (1,)), ((), ()))
TN = (((0,), (0,)), ((), ()))


def row_linkage(segment_ids):
    joined = segment_ids[..., 1:] == segment_ids[..., :-1]
    leading = jnp.zeros(segment_ids.shape[:-1] + (1,), jnp.float32)
    return jnp.concatenate([leading, joined.astype(jnp.float32)], axis=-1)


def wait_bytes(ref, sem):
    pltpu.make_async_copy(ref, ref, sem).wait()


def relay_kernel(
    n,
    sections,
    entering_ref,
    upstream_ref,
    link_ref,
    gain_ref,
    mix_ref,
    w_in_hbm,
    w_out_hbm,
    normed_ref,
    gate_ref,
    hidden_ref,
    up_ref,
    gain_out,
    mix_out,
    ag,
    part_out,
    part_in,
    sec_in,
    sec_out,
    w_in,
    w_out,
    summed_ref,
    hidden_grad,
    scale_ref,
    rate_out,
    rate_in,
    gain_acc,
    mix_acc,
    ag_send,
    ag_recv,
    rs_send,
    rs_recv,
    rate_send,
    rate_recv,
    sec_send,
    sec_recv,
    w_sem,
):
    me = lax.axis_index("tp")
    sec = lax.axis_index("section")
    micro, rows, width = entering_ref.shape
    tok = rows // 2
    lanes = rate_out.shape[-1]

    def load_in(j):
        return pltpu.make_async_copy(
            w_in_hbm.at[:, pl.ds(pl.multiple_of(j * width, width), width)],
            w_in.at[j],
            w_sem.at[0, j],
        )

    def load_out(j):
        return pltpu.make_async_copy(
            w_out_hbm.at[:, pl.ds(pl.multiple_of(j * width, width), width)],
            w_out.at[j],
            w_sem.at[1, j],
        )

    for j in range(n):
        load_in(j).start()
    for j in range(n):
        load_out(j).start()

    barrier = pltpu.get_barrier_semaphore()

    @pl.loop(1, n)
    def _(d):
        pl.semaphore_signal(
            barrier, inc=1, device_id={"tp": lax.rem(me + d, n)}, device_id_type=MESH
        )

    @pl.when(sec > 0)
    def _():
        pl.semaphore_signal(
            barrier, inc=1, device_id={"section": sec - 1}, device_id_type=MESH
        )

    @pl.when(sec < sections - 1)
    def _():
        pl.semaphore_signal(
            barrier, inc=1, device_id={"section": sec + 1}, device_id_type=MESH
        )

    outer = jnp.logical_or(sec == 0, sec == sections - 1)

    @pl.when(outer)
    def _():
        pl.semaphore_wait(barrier, n)

    @pl.when(jnp.logical_not(outer))
    def _():
        pl.semaphore_wait(barrier, n + 1)

    gain_acc[...] = jnp.zeros_like(gain_acc)
    mix_acc[...] = jnp.zeros_like(mix_acc)

    def gather_copy(phase, m, source, peer):
        return pltpu.make_async_remote_copy(
            src_ref=ag.at[phase, m, source],
            dst_ref=ag.at[phase, m, source],
            send_sem=ag_send.at[phase, m],
            recv_sem=ag_recv.at[phase, m, source],
            device_id={"tp": peer},
            device_id_type=MESH,
        )

    def part_copy(phase, m, peer):
        return pltpu.make_async_remote_copy(
            src_ref=part_out.at[phase, m, peer],
            dst_ref=part_in.at[phase, m, me],
            send_sem=rs_send.at[phase, m],
            recv_sem=rs_recv.at[phase, m],
            device_id={"tp": peer},
            device_id_type=MESH,
        )

    def rate_copy(m, peer):
        return pltpu.make_async_remote_copy(
            src_ref=rate_out.at[m],
            dst_ref=rate_in.at[m, me],
            send_sem=rate_send.at[m],
            recv_sem=rate_recv.at[m],
            device_id={"tp": peer},
            device_id_type=MESH,
        )

    def section_copy(phase, m, target):
        return pltpu.make_async_remote_copy(
            src_ref=sec_out.at[phase, m],
            dst_ref=sec_in.at[phase, m],
            send_sem=sec_send.at[phase, m],
            recv_sem=sec_recv.at[phase, m],
            device_id={"section": target},
            device_id_type=MESH,
        )

    def enter(phase, m, first, start_ref):
        @pl.when(first)
        def _():
            ag[phase, m, me] = start_ref[m]

        @pl.when(jnp.logical_not(first))
        def _():
            section_copy(phase, m, sec).wait_recv()
            ag[phase, m, me] = sec_in[phase, m]

        @pl.loop(1, n)
        def _(d):
            gather_copy(phase, m, me, lax.rem(me + d, n)).start()

    def arrive(phase, m, d):
        source = lax.rem(me - d + n, n)

        @pl.when(d > 0)
        def _():
            gather_copy(phase, m, source, me).wait_recv()

        return source

    def reduced(phase, m):
        wait_bytes(part_in.at[phase, m, pl.ds(0, n - 1)], rs_recv.at[phase, m])
        own = part_out[phase, m, me].astype(jnp.float32)

        def add(d, total):
            return total + part_in[phase, m, lax.rem(me + d, n)].astype(jnp.float32)

        return lax.fori_loop(1, n, add, own)

    def store_rows(ref, m, values):
        start = pl.multiple_of(m * tok, tok)
        for p in range(2):
            ref[p, pl.ds(start, tok), :] = values[p * tok : (p + 1) * tok]

    def mixed(m, source):
        floats = ag[0, m, source].astype(jnp.float32)
        earlier = pltpu.roll(floats, 1, 0) * link_ref[m]
        delta = earlier - floats
        return floats, delta, floats + mix_ref[source] * delta

    def forward(m):
        enter(0, m, sec == 0, entering_ref)
        summed_ref[m] = jnp.zeros_like(summed_ref[m])

        def gather_step(d, squares):
            source = arrive(0, m, d)

            @pl.when(m == 0)
            def _():
                load_in(source).wait()

            _, _, united = mixed(m, source)
            normed = (united * gain_ref[source]).astype(jnp.bfloat16)
            store_rows(normed_ref.at[source], m, normed)
            summed_ref[m] += lax.dot_general(
                normed, w_in[source], NT, preferred_element_type=jnp.float32
            )
            return squares + jnp.sum(united * united, axis=-1, keepdims=True)

        squares = lax.fori_loop(0, n, gather_step, jnp.zeros((rows, 1), jnp.float32))
        row_scale = lax.rsqrt(squares / (n * width) + epsilon)
        scale_ref[m] = jnp.broadcast_to(row_scale, scale_ref.shape[1:])
        pre_act = row_scale * summed_ref[m]
        hidden = (pre_act / (1.0 + jnp.exp(-pre_act))).astype(jnp.bfloat16)
        store_rows(hidden_ref, m, hidden)

        def part(target):
            @pl.when(m == 0)
            def _():
                load_out(target).wait()

            rows_in = jnp.concatenate(
                [hidden_ref[p, pl.ds(pl.multiple_of(m * tok, tok), tok), :] for p in range(2)]
            )
            part_out[0, m, target] = jnp.dot(
                rows_in, w_out[target], preferred_element_type=jnp.float32
            ).astype(jnp.bfloat16)

        @pl.loop(1, n)
        def _(d):
            target = lax.rem(me + d, n)
            part(target)
            part_copy(0, m, target).start()

        part(me)
        below = ag[0, m, me].astype(jnp.float32) + reduced(0, m)
        sec_out[0, m] = below.astype(jnp.bfloat16)

        @pl.when(sec < sections - 1)
        def _():
            section_copy(0, m, sec + 1).start()

    def backward(m):
        enter(1, m, sec == sections - 1, upstream_ref)
        hidden_grad[...] = jnp.zeros_like(hidden_grad)

        @pl.loop(0, n)
        def _(d):
            source = arrive(1, m, d)
            values = ag[1, m, source]
            store_rows(up_ref.at[source], m, values)
            hidden_grad[...] += lax.dot_general(
                values, w_out[source], NT, preferred_element_type=jnp.float32
            )

        row_scale = scale_ref[m][:, :1]
        summed = summed_ref[m]
        pre_act = row_scale * summed
        sigmoid = 1.0 / (1.0 + jnp.exp(-pre_act))
        gate_grad = hidden_grad[...] * (sigmoid * (1.0 + pre_act * (1.0 - sigmoid)))
        store_rows(gate_ref, m, (gate_grad * row_scale).astype(jnp.bfloat16))
        rate = jnp.sum(gate_grad * summed, axis=-1, keepdims=True)
        diagonal = lax.broadcasted_iota(jnp.int32, (rows, lanes), 0) == lax.broadcasted_iota(
            jnp.int32, (rows, lanes), 1
        )
        rate_row = jnp.sum(jnp.where(diagonal, rate, 0.0), axis=0, keepdims=True)
        rate_out[m] = jnp.broadcast_to(rate_row, rate_out.shape[1:])

        @pl.loop(1, n)
        def _(d):
            rate_copy(m, lax.rem(me + d, n)).start()

        def part(target):
            rows_in = jnp.concatenate(
                [gate_ref[p, pl.ds(pl.multiple_of(m * tok, tok), tok), :] for p in range(2)]
            )
            part_out[1, m, target] = jnp.dot(
                rows_in, w_in[target], preferred_element_type=jnp.float32
            ).astype(jnp.bfloat16)

        @pl.loop(1, n)
        def _(d):
            target = lax.rem(me + d, n)
            part(target)
            part_copy(1, m, target).start()

        part(me)
        wait_bytes(rate_in.at[m, pl.ds(0, n - 1)], rate_recv.at[m])

        def add_rate(d, total):
            return total + rate_in[m, lax.rem(me + d, n)]

        rates = lax.fori_loop(1, n, add_rate, rate_out[m])
        grad_rate = jnp.sum(jnp.where(diagonal, rates[:1], 0.0), axis=-1, keepdims=True)
        grad_normed = reduced(1, m)
        _, delta, united = mixed(m, me)
        mix = mix_ref[me]
        factor = grad_rate * (row_scale * row_scale * row_scale) / (n * width)
        grad_united = grad_normed * gain_ref[me] - factor * united
        gain_rows = grad_normed * united
        mix_rows = grad_united * delta
        for p in range(2):
            own = slice(p * tok, (p + 1) * tok)
            gain_acc[p] += jnp.sum(gain_rows[own], axis=0, keepdims=True)
            mix_acc[p] += jnp.sum(mix_rows[own], axis=0, keepdims=True)
        later = pltpu.roll(link_ref[m] * (grad_united * mix), rows - 1, 0)
        below = ag[1, m, me].astype(jnp.float32) + grad_united * (1.0 - mix) + later
        sec_out[1, m] = below.astype(jnp.bfloat16)

        @pl.when(sec > 0)
        def _():
            section_copy(1, m, sec - 1).start()

    @pl.loop(0, micro)
    def _(m):
        forward(m)

    @pl.loop(0, micro)
    def _(m):
        backward(m)

    def twice_rounded(acc):
        return acc[0].astype(jnp.bfloat16).astype(jnp.float32) + acc[1].astype(
            jnp.bfloat16
        ).astype(jnp.float32)

    gain_out[...] = twice_rounded(gain_acc)
    mix_out[...] = twice_rounded(mix_acc)

    @pl.loop(0, micro)
    def _(m):
        for phase in range(2):
            wait_bytes(ag.at[phase, m, pl.ds(0, n - 1)], ag_send.at[phase, m])
            wait_bytes(part_out.at[phase, m, pl.ds(0, n - 1)], rs_send.at[phase, m])
        wait_bytes(rate_in.at[m, pl.ds(0, n - 1)], rate_send.at[m])

        @pl.when(sec < sections - 1)
        def _():
            section_copy(0, m, sec).wait_send()

        @pl.when(sec > 0)
        def _():
            section_copy(1, m, sec).wait_send()


def grads_kernel(normed_ref, gate_ref, hidden_ref, up_ref, grad_in_ref, grad_out_ref):
    def summed(left, right):
        pair = [
            lax.dot_general(left[p], right[p], TN, preferred_element_type=jnp.float32)
            .astype(jnp.bfloat16)
            .astype(jnp.float32)
            for p in range(2)
        ]
        return (pair[0] + pair[1]).astype(jnp.bfloat16)

    grad_in_ref[0] = summed(gate_ref, normed_ref[0])
    grad_out_ref[0] = summed(hidden_ref, up_ref[0])


def local(
    entering, output_grad, live_counts, segment_ids, weight_in, weight_out, norm_gain, shift_mix
):
    sections = lax.axis_size("section")
    n = lax.axis_size("tp")
    relays, micro, tok, width = entering.shape
    rows = relays * tok
    hidden = weight_in.shape[2]
    width_all = weight_in.shape[1]
    lanes = -(-rows // 128) * 128
    linkage = row_linkage(segment_ids)
    live_rows = jnp.arange(tok)[None, None, :] < live_counts[..., None]
    upstream = jnp.where(live_rows[..., None], output_grad, jnp.zeros_like(output_grad))

    def by_micro(values):
        return jnp.swapaxes(values, 0, 1).reshape((micro, rows) + values.shape[3:])

    bf16, f32 = jnp.bfloat16, jnp.float32
    vmem = pl.BlockSpec(memory_space=pltpu.VMEM)
    hbm = pl.BlockSpec(memory_space=pl.ANY)
    dma = pltpu.SemaphoreType.DMA
    normed, gate, hidden_rows, up, gain, mix = pl.pallas_call(
        functools.partial(relay_kernel, n, sections),
        out_shape=(
            jax.ShapeDtypeStruct((n, 2, micro * tok, width), bf16),
            jax.ShapeDtypeStruct((2, micro * tok, hidden), bf16),
            jax.ShapeDtypeStruct((2, micro * tok, hidden), bf16),
            jax.ShapeDtypeStruct((n, 2, micro * tok, width), bf16),
            jax.ShapeDtypeStruct((1, width), f32),
            jax.ShapeDtypeStruct((1, width), f32),
        ),
        in_specs=[vmem] * 5 + [hbm] * 2,
        out_specs=(vmem,) * 6,
        scratch_shapes=[
            pltpu.VMEM((2, micro, n, rows, width), bf16),
            pltpu.VMEM((2, micro, n, rows, width), bf16),
            pltpu.VMEM((2, micro, n, rows, width), bf16),
            pltpu.VMEM((2, micro, rows, width), bf16),
            pltpu.VMEM((2, micro, rows, width), bf16),
            pltpu.VMEM((n, hidden, width), bf16),
            pltpu.VMEM((n, hidden, width), bf16),
            pltpu.VMEM((micro, rows, hidden), f32),
            pltpu.VMEM((rows, hidden), f32),
            pltpu.VMEM((micro, rows, 128), f32),
            pltpu.VMEM((micro, 8, lanes), f32),
            pltpu.VMEM((micro, n, 8, lanes), f32),
            pltpu.VMEM((2, 1, width), f32),
            pltpu.VMEM((2, 1, width), f32),
            dma((2, micro)),
            dma((2, micro, n)),
            dma((2, micro)),
            dma((2, micro)),
            dma((micro,)),
            dma((micro,)),
            dma((2, micro)),
            dma((2, micro)),
            dma((2, n)),
        ],
        compiler_params=pltpu.CompilerParams(
            collective_id=0, has_side_effects=True, vmem_limit_bytes=60 * 1024 * 1024
        ),
        name="relays",
    )(
        by_micro(entering),
        by_micro(upstream),
        by_micro(linkage)[..., None],
        norm_gain[0].astype(f32).reshape(n, 1, width),
        shift_mix[0].astype(f32).reshape(n, 1, width),
        jnp.swapaxes(weight_in[0], 0, 1),
        weight_out[0],
    )

    total = micro * tok
    part = pl.BlockSpec((1, 2, total, width), lambda j: (j, 0, 0, 0))
    whole = pl.BlockSpec((2, total, hidden), lambda j: (0, 0, 0))
    grad_in, grad_out = pl.pallas_call(
        grads_kernel,
        grid=(n,),
        out_shape=(
            jax.ShapeDtypeStruct((1, hidden, width_all), bf16),
            jax.ShapeDtypeStruct((1, hidden, width_all), bf16),
        ),
        in_specs=[part, whole, whole, part],
        out_specs=(
            pl.BlockSpec((1, hidden, width), lambda j: (0, 0, j)),
            pl.BlockSpec((1, hidden, width), lambda j: (0, 0, j)),
        ),
        compiler_params=pltpu.CompilerParams(
            dimension_semantics=("arbitrary",), vmem_limit_bytes=60 * 1024 * 1024
        ),
        name="weight_grads",
    )(normed, gate, hidden_rows, up)
    return jnp.swapaxes(grad_in, 1, 2), grad_out, gain, mix


def solution(mesh):
    in_specs = (
        P(None, None, None, "tp"),
        P(None, None, None, "tp"),
        P(),
        P(),
        P("section", None, "tp"),
        P("section", "tp", None),
        P("section", None),
        P("section", None),
    )
    out_specs = (
        P("section", None, "tp"),
        P("section", "tp", None),
        P("section", "tp"),
        P("section", "tp"),
    )
    return jax.shard_map(local, mesh=mesh, in_specs=in_specs, out_specs=out_specs, check_vma=False)
```

time: 1130 us -> 388 us (0.34)
  waiting for transfers between devices: 417 us -> 0 us
  Pallas kernels: 0 us -> 374 us
  blocking collectives: 266 us -> 0 us
  matrix products: 189 us -> 0 us
  other arithmetic: 169 us -> 5.35 us
  local copies, waits for them, and re-layouts: 35.2 us -> 5.57 us
  starting transfers between devices: 28.1 us -> 0 us
  between operations: 14.1 us -> 0.65 us
    reduce_scatter x12 -> x0, waiting for transfers between devices: 381 us -> none  [the longest x6 231 us: forward_tick(): lax.psum_scatter(jnp.stack(partial_list).astype(jnp.bfloat16), 'tp', scat...]
    pallas_call x0 -> x2, Pallas kernels: none -> 374 us  [the longest x1 358 us: local(): pl.pallas_call(functools.partial(relay_kernel, n, sections), out_shape=(j...]
    dot_general x28 -> x0, matrix products: 189 us -> none  [the longest x6 46.1 us: backward_tick(): lax.dot_general(gate_rows, first_weights, (((1,), (1,)), ((), ())), prefe...]
    all_gather x12 -> x0, blocking collectives: 180 us -> none  [the longest x6 90.9 us: forward_tick(): lax.all_gather(shortened(jnp.stack(shards)), 'tp', axis=2, tiled=True)]
    psum x6 -> x0, blocking collectives: 85.8 us -> none  [backward_tick(): grad_rate = lax.psum(jnp.stack(rate_list), 'tp')]
    scatter x72 -> x0, other arithmetic: 83 us -> none  [write_slot(): buffer.at[relay, slot_index].set(jnp.where(active_now, values, current))]
    another operation x80 -> x1, other arithmetic: 36.8 us -> 0.08 us  [local(): by_micro(linkage)[..., None]]
    ppermute x12 -> x0, waiting for transfers between devices: 36.1 us -> none  [passed_along(): lax.ppermute(value, axis, [(source, source + steps) for source in range(l...]
  transfers between devices with their start and end apart: 24 -> 0, of which waited for: 24 -> 0; matrix products, arithmetic and copies ran while one was open for 5% -> 0% of each run, Pallas kernels for 0% -> 0%
where the time goes in v1:
time: 388 us; the launch traced here: 386 us
  Pallas kernels  374 us (96%)
  local copies, waits for them, and re-layouts  5.57 us (1%)
  other arithmetic  5.35 us (1%)
    pallas_call x1, Pallas kernels, local(): pl.pallas_call(functools.partial(relay_kernel, n, sections), out_shape=(j...  358 us
    pallas_call x1, Pallas kernels, local(): pl.pallas_call(grads_kernel, grid=(n,), out_shape=(jax.ShapeDtypeStruct((...  16 us

profile of v1, /device:TPU:0, one launch (start us, length us, event | category | flops | bytes accessed | tf_op | source)
XLA Modules:
  0.0 385.7 jit_solution(10832646772818786363)
XLA Ops:
  0.6 0.8 iota_compare_fusion
  1.4 0.8 slice_compare_fusion
  2.2 0.1 fusion
  2.3 1.3 convert.6.gain_ref
  3.6 1.3 convert.7.mix_ref
  5.0 0.8 reshape.49.link_ref
  5.7 1.0 select_bitcast_fusion
  6.7 0.7 copy.15
  7.4 1.6 copy.14
  9.0 358.1 %relays.1 = (bf16[8,2,96,512]{3,2,1,0:T(8,128)(2,1)}, bf16[2,96,1376]{2,1,0:T(8,128)(2,1)}, bf16[2,96,1376]{2,1,0:T(8,128)(2,1)}, bf16[8,2,96,512]{3,2,1,0:T(8,1...) custom-call(bf16[3,64,512]{2,1,0:T(8,128)(2,1)} %bitcast.19, bf16[3,64,512]{2,1,0:T(8,128)(2,1)} %bitcast.18, ...), custom_call_target="tpu_custom_call" | custom-call | tf_op jit(solution)/shard_map/relays/pallas_call | solution.py:397
  367.1 16.0 %weight_grads.1 = (bf16[1,1376,4096]{2,1,0:T(8,128)(2,1)}, bf16[1,1376,4096]{2,1,0:T(8,128)(2,1)}) custom-call(bf16[8,2,96,512]{3,2,1,0:T(8,128)(2,1)} %get-tuple-element.12.normed_ref, bf16[2,96,1376]{2,1,0:T(8,128)(2,1)} %get-tuple-element.13.gate_ref, bf16[2,96,1376]{2,1,0:T(8,128)(2,1)} %get-tuple-element.14.hidden_ref, ...), custom_call_target="tpu_custom_call" | custom-call | tf_op jit(solution)/shard_map/weight_grads/pallas_call | solution.py:451
  383.2 1.3 copy.19
  384.4 1.3 copy.20

commit v2 on v1

--- a/solution.py
+++ b/solution.py
@@ -13,12 +13,6 @@
 TN = (((0,), (0,)), ((), ()))
 
 
-def row_linkage(segment_ids):
-    joined = segment_ids[..., 1:] == segment_ids[..., :-1]
-    leading = jnp.zeros(segment_ids.shape[:-1] + (1,), jnp.float32)
-    return jnp.concatenate([leading, joined.astype(jnp.float32)], axis=-1)
-
-
 def wait_bytes(ref, sem):
     pltpu.make_async_copy(ref, ref, sem).wait()
 
@@ -26,24 +20,30 @@
 def relay_kernel(
     n,
     sections,
+    live_ref,
     entering_ref,
     upstream_ref,
-    link_ref,
-    gain_ref,
-    mix_ref,
+    segment_ref,
+    gain_row,
+    mix_row,
     w_in_hbm,
     w_out_hbm,
     normed_ref,
     gate_ref,
     hidden_ref,
     up_ref,
-    gain_out,
-    mix_out,
+    gain_acc,
+    mix_acc,
     ag,
+    pair_out,
+    pair_in,
     part_out,
     part_in,
-    sec_in,
     sec_out,
+    link_ref,
+    live_rows,
+    gain_ref,
+    mix_ref,
     w_in,
     w_out,
     summed_ref,
@@ -51,10 +51,10 @@
     scale_ref,
     rate_out,
     rate_in,
-    gain_acc,
-    mix_acc,
     ag_send,
     ag_recv,
+    pair_send,
+    pair_recv,
     rs_send,
     rs_recv,
     rate_send,
@@ -65,8 +65,13 @@
 ):
     me = lax.axis_index("tp")
     sec = lax.axis_index("section")
-    micro, rows, width = entering_ref.shape
-    tok = rows // 2
+    _, micro, tok, width = entering_ref.shape
+    rows = 2 * tok
+    chips = n // 2
+    chip = me // 2
+    core = lax.rem(me, 2)
+    sibling = me + 1 - 2 * core
+    last = sections - 1
     lanes = rate_out.shape[-1]
 
     def load_in(j):
@@ -87,6 +92,24 @@
         load_in(j).start()
     for j in range(n):
         load_out(j).start()
+
+    square = [lax.broadcasted_iota(jnp.int32, (tok, tok), axis) for axis in range(2)]
+    column = lax.broadcasted_iota(jnp.int32, (tok, 1), 0)
+    for p in range(2):
+        for m in range(micro):
+            own = slice(p * tok, (p + 1) * tok)
+            ids = segment_ref[p, m : m + 1, :].astype(jnp.float32)
+            here = jnp.sum(jnp.where(square[0] == square[1], ids, 0.0), axis=-1, keepdims=True)
+            before = jnp.sum(
+                jnp.where(square[0] == square[1] + 1, ids, 0.0), axis=-1, keepdims=True
+            )
+            joined = jnp.logical_and(here == before, column > 0)
+            link_ref[m, own, :] = jnp.where(joined, 1.0, 0.0)
+            live_rows[m, own, :] = jnp.where(column < live_ref[p, m], 1.0, 0.0)
+    for j in range(n):
+        own = slice(j * width, (j + 1) * width)
+        gain_ref[j] = gain_row[:, own].astype(jnp.float32)
+        mix_ref[j] = mix_row[:, own].astype(jnp.float32)
 
     barrier = pltpu.get_barrier_semaphore()
 
@@ -131,13 +154,23 @@
             device_id_type=MESH,
         )
 
-    def part_copy(phase, m, peer):
+    def pair_copy(phase, m, target):
         return pltpu.make_async_remote_copy(
-            src_ref=part_out.at[phase, m, peer],
-            dst_ref=part_in.at[phase, m, me],
+            src_ref=pair_out.at[phase, m, target],
+            dst_ref=pair_in.at[phase, m, target],
+            send_sem=pair_send.at[phase, m],
+            recv_sem=pair_recv.at[phase, m, target],
+            device_id={"tp": sibling},
+            device_id_type=MESH,
+        )
+
+    def part_copy(phase, m, target):
+        return pltpu.make_async_remote_copy(
+            src_ref=part_out.at[phase, m, target],
+            dst_ref=part_in.at[phase, m, chip],
             send_sem=rs_send.at[phase, m],
             recv_sem=rs_recv.at[phase, m],
-            device_id={"tp": peer},
+            device_id={"tp": 2 * target + core},
             device_id_type=MESH,
         )
 
@@ -154,44 +187,87 @@
     def section_copy(phase, m, target):
         return pltpu.make_async_remote_copy(
             src_ref=sec_out.at[phase, m],
-            dst_ref=sec_in.at[phase, m],
+            dst_ref=ag.at[phase, m, me],
             send_sem=sec_send.at[phase, m],
             recv_sem=sec_recv.at[phase, m],
             device_id={"section": target},
             device_id_type=MESH,
         )
 
-    def enter(phase, m, first, start_ref):
-        @pl.when(first)
-        def _():
-            ag[phase, m, me] = start_ref[m]
-
-        @pl.when(jnp.logical_not(first))
-        def _():
-            section_copy(phase, m, sec).wait_recv()
-            ag[phase, m, me] = sec_in[phase, m]
-
-        @pl.loop(1, n)
-        def _(d):
-            gather_copy(phase, m, me, lax.rem(me + d, n)).start()
+    def spread(phase, m):
+        @pl.loop(1, chips)
+        def _(k):
+            gather_copy(phase, m, me, 2 * lax.rem(chip + k, chips) + core).start()
+
+        gather_copy(phase, m, me, sibling).start()
+
+    def enter_forward(m):
+        @pl.when(sec == 0)
+        def _():
+            for p in range(2):
+                ag[0, m, me, p * tok : (p + 1) * tok, :] = entering_ref[p, m]
+
+        @pl.when(sec > 0)
+        def _():
+            section_copy(0, m, sec).wait_recv()
+
+        spread(0, m)
 
     def arrive(phase, m, d):
-        source = lax.rem(me - d + n, n)
+        k = d // 2
+        other = lax.rem(d, 2)
+        source = 2 * lax.rem(chip - k + chips, chips) + core + other * (1 - 2 * core)
 
         @pl.when(d > 0)
         def _():
             gather_copy(phase, m, source, me).wait_recv()
 
+        @pl.when(jnp.logical_and(d > 0, other == 0))
+        def _():
+            gather_copy(phase, m, source, sibling).start()
+
         return source
 
+    def scatter(phase, m, values_ref, weights):
+        start = pl.multiple_of(m * tok, tok)
+        values = jnp.concatenate([values_ref[p, pl.ds(start, tok), :] for p in range(2)])
+        skew = min(2, chips)
+
+        @pl.loop(0, chips + skew)
+        def _(i):
+            @pl.when(i < chips)
+            def _():
+                target = lax.rem(chip + 1 + i, chips)
+                pair_out[phase, m, target] = jnp.dot(
+                    values,
+                    weights[2 * target + 1 - core],
+                    preferred_element_type=jnp.float32,
+                ).astype(jnp.bfloat16)
+                pair_copy(phase, m, target).start()
+
+            @pl.when(i >= skew)
+            def _():
+                target = lax.rem(chip + 1 + i - skew + chips, chips)
+                own = jnp.dot(
+                    values, weights[2 * target + core], preferred_element_type=jnp.float32
+                )
+                pair_copy(phase, m, target).wait_recv()
+                part_out[phase, m, target] = (
+                    own + pair_in[phase, m, target].astype(jnp.float32)
+                ).astype(jnp.bfloat16)
+
+                @pl.when(i < chips + skew - 1)
+                def _():
+                    part_copy(phase, m, target).start()
+
     def reduced(phase, m):
-        wait_bytes(part_in.at[phase, m, pl.ds(0, n - 1)], rs_recv.at[phase, m])
-        own = part_out[phase, m, me].astype(jnp.float32)
-
-        def add(d, total):
-            return total + part_in[phase, m, lax.rem(me + d, n)].astype(jnp.float32)
-
-        return lax.fori_loop(1, n, add, own)
+        wait_bytes(part_in.at[phase, m, pl.ds(0, chips - 1)], rs_recv.at[phase, m])
+        own = part_out[phase, m, chip].astype(jnp.float32)
+
+        def add(k, total):
+            return total + part_in[phase, m, lax.rem(chip + k, chips)].astype(jnp.float32)
+
+        return lax.fori_loop(1, chips, add, own)
 
     def store_rows(ref, m, values):
         start = pl.multiple_of(m * tok, tok)
@@ -205,7 +281,6 @@
         return floats, delta, floats + mix_ref[source] * delta
 
     def forward(m):
-        enter(0, m, sec == 0, entering_ref)
         summed_ref[m] = jnp.zeros_like(summed_ref[m])
 
         def gather_step(d, squares):
@@ -230,34 +305,40 @@
         hidden = (pre_act / (1.0 + jnp.exp(-pre_act))).astype(jnp.bfloat16)
         store_rows(hidden_ref, m, hidden)
 
-        def part(target):
-            @pl.when(m == 0)
-            def _():
-                load_out(target).wait()
-
-            rows_in = jnp.concatenate(
-                [hidden_ref[p, pl.ds(pl.multiple_of(m * tok, tok), tok), :] for p in range(2)]
-            )
-            part_out[0, m, target] = jnp.dot(
-                rows_in, w_out[target], preferred_element_type=jnp.float32
-            ).astype(jnp.bfloat16)
-
-        @pl.loop(1, n)
-        def _(d):
-            target = lax.rem(me + d, n)
-            part(target)
-            part_copy(0, m, target).start()
-
-        part(me)
+        @pl.when(m == 0)
+        def _():
+            for j in range(n):
+                load_out(j).wait()
+
+        @pl.when(sec < last)
+        def _():
+            scatter(0, m, hidden_ref, w_out)
+
+    def finish_forward(m):
         below = ag[0, m, me].astype(jnp.float32) + reduced(0, m)
         sec_out[0, m] = below.astype(jnp.bfloat16)
-
-        @pl.when(sec < sections - 1)
-        def _():
-            section_copy(0, m, sec + 1).start()
+        section_copy(0, m, sec + 1).start()
+
+    def enter_backward(m):
+        @pl.when(sec == last)
+        def _():
+            for p in range(2):
+                own = slice(p * tok, (p + 1) * tok)
+                ag[1, m, me, own, :] = (
+                    upstream_ref[p, m].astype(jnp.float32) * live_rows[m, own, :]
+                ).astype(jnp.bfloat16)
+
+        @pl.when(sec < last)
+        def _():
+            section_copy(1, m, sec).wait_recv()
+
+        spread(1, m)
+
+    diagonal = lax.broadcasted_iota(jnp.int32, (rows, lanes), 0) == lax.broadcasted_iota(
+        jnp.int32, (rows, lanes), 1
+    )
 
     def backward(m):
-        enter(1, m, sec == sections - 1, upstream_ref)
         hidden_grad[...] = jnp.zeros_like(hidden_grad)
 
         @pl.loop(0, n)
@@ -276,9 +357,6 @@
         gate_grad = hidden_grad[...] * (sigmoid * (1.0 + pre_act * (1.0 - sigmoid)))
         store_rows(gate_ref, m, (gate_grad * row_scale).astype(jnp.bfloat16))
         rate = jnp.sum(gate_grad * summed, axis=-1, keepdims=True)
-        diagonal = lax.broadcasted_iota(jnp.int32, (rows, lanes), 0) == lax.broadcasted_iota(
-            jnp.int32, (rows, lanes), 1
-        )
         rate_row = jnp.sum(jnp.where(diagonal, rate, 0.0), axis=0, keepdims=True)
         rate_out[m] = jnp.broadcast_to(rate_row, rate_out.shape[1:])
 
@@ -286,21 +364,10 @@
         def _(d):
             rate_copy(m, lax.rem(me + d, n)).start()
 
-        def part(target):
-            rows_in = jnp.concatenate(
-                [gate_ref[p, pl.ds(pl.multiple_of(m * tok, tok), tok), :] for p in range(2)]
-            )
-            part_out[1, m, target] = jnp.dot(
-                rows_in, w_in[target], preferred_element_type=jnp.float32
-            ).astype(jnp.bfloat16)
-
-        @pl.loop(1, n)
-        def _(d):
-            target = lax.rem(me + d, n)
-            part(target)
-            part_copy(1, m, target).start()
-
-        part(me)
+        scatter(1, m, gate_ref, w_in)
+
+    def finish_backward(m):
+        row_scale = scale_ref[m][:, :1]
         wait_bytes(rate_in.at[m, pl.ds(0, n - 1)], rate_recv.at[m])
 
         def add_rate(d, total):
@@ -327,31 +394,54 @@
         def _():
             section_copy(1, m, sec - 1).start()
 
+    enter_forward(0)
+
+    @pl.when(sec == last)
+    def _():
+        @pl.loop(0, micro)
+        def _(m):
+            enter_backward(m)
+
     @pl.loop(0, micro)
     def _(m):
         forward(m)
 
+        @pl.when(m < micro - 1)
+        def _():
+            enter_forward(m + 1)
+
+        @pl.when(sec < last)
+        def _():
+            finish_forward(m)
+
+    @pl.when(sec < last)
+    def _():
+        enter_backward(0)
+
     @pl.loop(0, micro)
     def _(m):
         backward(m)
 
-    def twice_rounded(acc):
-        return acc[0].astype(jnp.bfloat16).astype(jnp.float32) + acc[1].astype(
-            jnp.bfloat16
-        ).astype(jnp.float32)
-
-    gain_out[...] = twice_rounded(gain_acc)
-    mix_out[...] = twice_rounded(mix_acc)
+        @pl.when(jnp.logical_and(m < micro - 1, sec < last))
+        def _():
+            enter_backward(m + 1)
+
+        finish_backward(m)
 
     @pl.loop(0, micro)
     def _(m):
+        def sent(phase):
+            wait_bytes(pair_out.at[phase, m], pair_send.at[phase, m])
+            wait_bytes(part_out.at[phase, m, pl.ds(0, chips - 1)], rs_send.at[phase, m])
+
         for phase in range(2):
             wait_bytes(ag.at[phase, m, pl.ds(0, n - 1)], ag_send.at[phase, m])
-            wait_bytes(part_out.at[phase, m, pl.ds(0, n - 1)], rs_send.at[phase, m])
+        sent(1)
         wait_bytes(rate_in.at[m, pl.ds(0, n - 1)], rate_send.at[m])
 
-        @pl.when(sec < sections - 1)
-        def _():
+        @pl.when(sec < last)
+        def _():
+            sent(0)
             section_copy(0, m, sec).wait_send()
 
         @pl.when(sec > 0)
@@ -359,18 +449,21 @@
             section_copy(1, m, sec).wait_send()
 
 
-def grads_kernel(normed_ref, gate_ref, hidden_ref, up_ref, grad_in_ref, grad_out_ref):
+def grads_kernel(
+    normed_ref, gate_ref, hidden_ref, up_ref, gain_ref, mix_ref, grad_in, grad_out, gain, mix
+):
     def summed(left, right):
-        pair = [
-            lax.dot_general(left[p], right[p], TN, preferred_element_type=jnp.float32)
-            .astype(jnp.bfloat16)
-            .astype(jnp.float32)
-            for p in range(2)
-        ]
-        return (pair[0] + pair[1]).astype(jnp.bfloat16)
-
-    grad_in_ref[0] = summed(gate_ref, normed_ref[0])
-    grad_out_ref[0] = summed(hidden_ref, up_ref[0])
+        left, right = [v.reshape((-1, v.shape[-1])) for v in (left, right)]
+        return lax.dot_general(left, right, TN, preferred_element_type=jnp.float32)
+
+    def twice_rounded(acc):
+        pair = [acc[p].astype(jnp.bfloat16).astype(jnp.float32) for p in range(2)]
+        return pair[0] + pair[1]
+
+    grad_in[0] = summed(gate_ref[...], normed_ref[0]).astype(grad_in.dtype)
+    grad_out[0] = summed(hidden_ref[...], up_ref[0]).astype(grad_out.dtype)
+    gain[...] = twice_rounded(gain_ref)
+    mix[...] = twice_rounded(mix_ref)
 
 
 def local(
@@ -383,35 +476,34 @@
     hidden = weight_in.shape[2]
     width_all = weight_in.shape[1]
     lanes = -(-rows // 128) * 128
-    linkage = row_linkage(segment_ids)
-    live_rows = jnp.arange(tok)[None, None, :] < live_counts[..., None]
-    upstream = jnp.where(live_rows[..., None], output_grad, jnp.zeros_like(output_grad))
-
-    def by_micro(values):
-        return jnp.swapaxes(values, 0, 1).reshape((micro, rows) + values.shape[3:])
-
     bf16, f32 = jnp.bfloat16, jnp.float32
     vmem = pl.BlockSpec(memory_space=pltpu.VMEM)
+    smem = pl.BlockSpec(memory_space=pltpu.SMEM)
     hbm = pl.BlockSpec(memory_space=pl.ANY)
     dma = pltpu.SemaphoreType.DMA
-    normed, gate, hidden_rows, up, gain, mix = pl.pallas_call(
+    normed, gate, hidden_rows, up, gain_sums, mix_sums = pl.pallas_call(
         functools.partial(relay_kernel, n, sections),
         out_shape=(
             jax.ShapeDtypeStruct((n, 2, micro * tok, width), bf16),
             jax.ShapeDtypeStruct((2, micro * tok, hidden), bf16),
             jax.ShapeDtypeStruct((2, micro * tok, hidden), bf16),
             jax.ShapeDtypeStruct((n, 2, micro * tok, width), bf16),
-            jax.ShapeDtypeStruct((1, width), f32),
-            jax.ShapeDtypeStruct((1, width), f32),
+            jax.ShapeDtypeStruct((2, 1, width), f32),
+            jax.ShapeDtypeStruct((2, 1, width), f32),
         ),
-        in_specs=[vmem] * 5 + [hbm] * 2,
+        in_specs=[smem] + [vmem] * 5 + [hbm] * 2,
         out_specs=(vmem,) * 6,
         scratch_shapes=[
             pltpu.VMEM((2, micro, n, rows, width), bf16),
-            pltpu.VMEM((2, micro, n, rows, width), bf16),
-            pltpu.VMEM((2, micro, n, rows, width), bf16),
+            pltpu.VMEM((2, micro, n // 2, rows, width), bf16),
+            pltpu.VMEM((2, micro, n // 2, rows, width), bf16),
+            pltpu.VMEM((2, micro, n // 2, rows, width), bf16),
+            pltpu.VMEM((2, micro, n // 2, rows, width), bf16),
             pltpu.VMEM((2, micro, rows, width), bf16),
-            pltpu.VMEM((2, micro, rows, width), bf16),
+            pltpu.VMEM((micro, rows, 1), f32),
+            pltpu.VMEM((micro, rows, 1), f32),
+            pltpu.VMEM((n, 1, width), f32),
+            pltpu.VMEM((n, 1, width), f32),
             pltpu.VMEM((n, hidden, width), bf16),
             pltpu.VMEM((n, hidden, width), bf16),
             pltpu.VMEM((micro, rows, hidden), f32),
@@ -419,10 +511,10 @@
             pltpu.VMEM((micro, rows, 128), f32),
             pltpu.VMEM((micro, 8, lanes), f32),
             pltpu.VMEM((micro, n, 8, lanes), f32),
-            pltpu.VMEM((2, 1, width), f32),
-            pltpu.VMEM((2, 1, width), f32),
             dma((2, micro)),
             dma((2, micro, n)),
+            dma((2, micro)),
+            dma((2, micro, n // 2)),
             dma((2, micro)),
             dma((2, micro)),
             dma((micro,)),
@@ -436,11 +528,12 @@
         ),
         name="relays",
     )(
-        by_micro(entering),
-        by_micro(upstream),
-        by_micro(linkage)[..., None],
-        norm_gain[0].astype(f32).reshape(n, 1, width),
-        shift_mix[0].astype(f32).reshape(n, 1, width),
+        live_counts,
+        entering,
+        output_grad,
+        segment_ids,
+        norm_gain,
+        shift_mix,
         jnp.swapaxes(weight_in[0], 0, 1),
         weight_out[0],
     )
@@ -448,23 +541,29 @@
     total = micro * tok
     part = pl.BlockSpec((1, 2, total, width), lambda j: (j, 0, 0, 0))
     whole = pl.BlockSpec((2, total, hidden), lambda j: (0, 0, 0))
-    grad_in, grad_out = pl.pallas_call(
+    sums = pl.BlockSpec((2, 1, width), lambda j: (0, 0, 0))
+    row = pl.BlockSpec((1, width), lambda j: (0, 0))
+    grad_in, grad_out, gain, mix = pl.pallas_call(
         grads_kernel,
         grid=(n,),
         out_shape=(
             jax.ShapeDtypeStruct((1, hidden, width_all), bf16),
             jax.ShapeDtypeStruct((1, hidden, width_all), bf16),
+            jax.ShapeDtypeStruct((1, width), f32),
+            jax.ShapeDtypeStruct((1, width), f32),
         ),
-        in_specs=[part, whole, whole, part],
+        in_specs=[part, whole, whole, part, sums, sums],
         out_specs=(
             pl.BlockSpec((1, hidden, width), lambda j: (0, 0, j)),
             pl.BlockSpec((1, hidden, width), lambda j: (0, 0, j)),
+            row,
+            row,
         ),
         compiler_params=pltpu.CompilerParams(
             dimension_semantics=("arbitrary",), vmem_limit_bytes=60 * 1024 * 1024
         ),
         name="weight_grads",
-    )(normed, gate, hidden_rows, up)
+    )(normed, gate, hidden_rows, up, gain_sums, mix_sums)
     return jnp.swapaxes(grad_in, 1, 2), grad_out, gain, mix
 
 

time: 388 us -> 274 us (0.71)
  Pallas kernels: 374 us -> 271 us
  other arithmetic: 5.35 us -> 0 us
  local copies, waits for them, and re-layouts: 5.57 us -> 1.28 us
    pallas_call x1, Pallas kernels: 358 us -> 259 us  [local(): pl.pallas_call(functools.partial(relay_kernel, n, sections), out_shape=(j...]
    pallas_call x1, Pallas kernels: 16 us -> 12 us  [local(): pl.pallas_call(grads_kernel, grid=(n,), out_shape=(jax.ShapeDtypeStruct((...]
where the time goes in v2:
time: 274 us; the launch traced here: 273 us
  Pallas kernels  271 us (99%)
    pallas_call x1, Pallas kernels, local(): pl.pallas_call(functools.partial(relay_kernel, n, sections), out_shape=(j...  259 us
    pallas_call x1, Pallas kernels, local(): pl.pallas_call(grads_kernel, grid=(n,), out_shape=(jax.ShapeDtypeStruct((...  12 us

profile of v2, /device:TPU:0, one launch (start us, length us, event | category | flops | bytes accessed | tf_op | source)
XLA Modules:
  0.0 273.1 jit_solution(14497451179124926307)
XLA Ops:
  0.6 1.3 copy.12.segment_ref
  1.9 259.2 %relays.1 = (bf16[8,2,96,512]{3,2,1,0:T(8,128)(2,1)}, bf16[2,96,1376]{2,1,0:T(8,128)(2,1)}, bf16[2,96,1376]{2,1,0:T(8,128)(2,1)}, bf16[8,2,96,512]{3,2,1,0:T(8,1...) custom-call(s32[2,3]{1,0:T(2,128)} %live_ref.1, bf16[2,3,32,512]{3,2,1,0:T(8,128)(2,1)} %entering_ref.1, ...), custom_call_target="tpu_custom_call" | custom-call | tf_op jit(solution)/shard_map/relays/pallas_call | solution.py:484
  261.1 12.0 %weight_grads.1 = (bf16[1,1376,4096]{2,1,0:T(8,128)(2,1)}, bf16[1,1376,4096]{2,1,0:T(8,128)(2,1)}, f32[1,512]{1,0:T(1,128)}, f32[1,512]{1,0:T(1,128)}) custom-call(bf16[8,2,96,512]{3,2,1,0:T(8,128)(2,1)} %get-tuple-element.14.normed_ref, bf16[2,96,1376]{2,1,0:T(8,128)(2,1)} %get-tuple-element.15.gate_ref, bf16[2,96,1376]{2,1,0:T(8,128)(2,1)} %get-tuple-element.16.hidden_ref, ...), custom_call_target="tpu_custom_call" | custom-call | tf_op jit(solution)/shard_map/weight_grads/pallas_call | solution.py:546

commit v3 on v2

--- a/solution.py
+++ b/solution.py
@@ -305,7 +305,7 @@
         hidden = (pre_act / (1.0 + jnp.exp(-pre_act))).astype(jnp.bfloat16)
         store_rows(hidden_ref, m, hidden)
 
-        @pl.when(m == 0)
+        @pl.when(jnp.logical_and(m == 0, sec < last))
         def _():
             for j in range(n):
                 load_out(j).wait()
@@ -338,23 +338,25 @@
         jnp.int32, (rows, lanes), 1
     )
 
-    def backward(m):
-        hidden_grad[...] = jnp.zeros_like(hidden_grad)
+    def gather_backward(m):
+        hidden_grad[m] = jnp.zeros_like(hidden_grad[m])
 
         @pl.loop(0, n)
         def _(d):
             source = arrive(1, m, d)
             values = ag[1, m, source]
             store_rows(up_ref.at[source], m, values)
-            hidden_grad[...] += lax.dot_general(
+            hidden_grad[m] += lax.dot_general(
                 values, w_out[source], NT, preferred_element_type=jnp.float32
             )
+
+    def backward(m):
 
         row_scale = scale_ref[m][:, :1]
         summed = summed_ref[m]
         pre_act = row_scale * summed
         sigmoid = 1.0 / (1.0 + jnp.exp(-pre_act))
-        gate_grad = hidden_grad[...] * (sigmoid * (1.0 + pre_act * (1.0 - sigmoid)))
+        gate_grad = hidden_grad[m] * (sigmoid * (1.0 + pre_act * (1.0 - sigmoid)))
         store_rows(gate_ref, m, (gate_grad * row_scale).astype(jnp.bfloat16))
         rate = jnp.sum(gate_grad * summed, axis=-1, keepdims=True)
         rate_row = jnp.sum(jnp.where(diagonal, rate, 0.0), axis=0, keepdims=True)
@@ -402,6 +404,13 @@
         def _(m):
             enter_backward(m)
 
+        for j in range(n):
+            load_out(j).wait()
+
+        @pl.loop(0, micro)
+        def _(m):
+            gather_backward(m)
+
     @pl.loop(0, micro)
     def _(m):
         forward(m)
@@ -420,6 +429,10 @@
 
     @pl.loop(0, micro)
     def _(m):
+        @pl.when(sec < last)
+        def _():
+            gather_backward(m)
+
         backward(m)
 
         @pl.when(jnp.logical_and(m < micro - 1, sec < last))
@@ -507,7 +520,7 @@
             pltpu.VMEM((n, hidden, width), bf16),
             pltpu.VMEM((n, hidden, width), bf16),
             pltpu.VMEM((micro, rows, hidden), f32),
-            pltpu.VMEM((rows, hidden), f32),
+            pltpu.VMEM((micro, rows, hidden), f32),
             pltpu.VMEM((micro, rows, 128), f32),
             pltpu.VMEM((micro, 8, lanes), f32),
             pltpu.VMEM((micro, n, 8, lanes), f32),

time: 274 us -> 279 us (1.018)
  Pallas kernels: 271 us -> 276 us
    pallas_call x1, Pallas kernels: 259 us -> 264 us  [local(): pl.pallas_call(functools.partial(relay_kernel, n, sections), out_shape=(j...]
where the time goes in v3:
time: 279 us; the launch traced here: 278 us
  Pallas kernels  276 us (99%)
    pallas_call x1, Pallas kernels, local(): pl.pallas_call(functools.partial(relay_kernel, n, sections), out_shape=(j...  264 us
    pallas_call x1, Pallas kernels, local(): pl.pallas_call(grads_kernel, grid=(n,), out_shape=(jax.ShapeDtypeStruct((...  11.9 us

profile of v3, /device:TPU:0, one launch (start us, length us, event | category | flops | bytes accessed | tf_op | source)
XLA Modules:
  0.0 278.2 jit_solution(238505200018288148)
XLA Ops:
  0.6 1.3 copy.12.segment_ref
  1.9 264.3 %relays.1 = (bf16[8,2,96,512]{3,2,1,0:T(8,128)(2,1)}, bf16[2,96,1376]{2,1,0:T(8,128)(2,1)}, bf16[2,96,1376]{2,1,0:T(8,128)(2,1)}, bf16[8,2,96,512]{3,2,1,0:T(8,1...) custom-call(s32[2,3]{1,0:T(2,128)} %live_ref.1, bf16[2,3,32,512]{3,2,1,0:T(8,128)(2,1)} %entering_ref.1, ...), custom_call_target="tpu_custom_call" | custom-call | tf_op jit(solution)/shard_map/relays/pallas_call | solution.py:497
  266.3 11.9 %weight_grads.1 = (bf16[1,1376,4096]{2,1,0:T(8,128)(2,1)}, bf16[1,1376,4096]{2,1,0:T(8,128)(2,1)}, f32[1,512]{1,0:T(1,128)}, f32[1,512]{1,0:T(1,128)}) custom-call(bf16[8,2,96,512]{3,2,1,0:T(8,128)(2,1)} %get-tuple-element.14.normed_ref, bf16[2,96,1376]{2,1,0:T(8,128)(2,1)} %get-tuple-element.15.gate_ref, bf16[2,96,1376]{2,1,0:T(8,128)(2,1)} %get-tuple-element.16.hidden_ref, ...), custom_call_target="tpu_custom_call" | custom-call | tf_op jit(solution)/shard_map/weight_grads/pallas_call | solution.py:559
